TPU v7x, 32 devices: a whole 2x2x4 slice. The times are simulated.
32 devices in a mesh: groups: 1, row: 8 (over z, y), col: 4 (over x, core).
Axes of the slice: x: 2, y: 2, z: 4, core: 2. Of those that a mesh axis runs over, the one named last changes fastest.
Arguments:
- activations: bfloat16 [1024, 16384], P('groups', ('row', 'col')), may hold values from -2.5 to 2.5
- token_ids: int32 [1024], P('groups'), may hold values from 0 to 128255
- initial: float32 [16384, 256], P(('groups', 'row', 'col')), may hold values from -6 to 6
- block_mask: int32 [128, 2], P('groups'), may hold values 0 or 1
Outputs:
- gram: float32 [8, 4, 512, 16384], P('groups', 'col', None, 'row')
- repaired: float32 [16384, 256], P(('groups', 'row', 'col'))
All inputs are finite; a program needn't handle non-finite values.
Results may differ from a plain program's by a relative error of at most 0.0003.
Values may be sent and summed in bfloat16 or wider, within the bound.
No kernel may reach another device: no remote copies, remote signals or barrier semaphores. Data moves between devices by JAX's collectives and lax.ppermute only.
A program may use at most 128 MiB of HBM per device.

v0:
```python
import math
import jax
import jax.numpy as jnp
from jax import lax
from jax.sharding import PartitionSpec as P

D = 16384
ROWS = 1024
BLOCK = 128
ITERS = 2


def shards(activations, token_ids, initial, block_mask):
    matches = (token_ids[:, None] == token_ids[None, :]).astype(jnp.float32)
    weights = 1.0 / jnp.sum(matches, axis=1)
    weighted = (activations.astype(jnp.float32) * weights[:, None]).astype(jnp.bfloat16)
    column_panel = lax.all_gather(activations, "col", axis=1, tiled=True)
    gram_tile = lax.dot_general(
        lax.all_gather(weighted, "row", axis=1, tiled=True),
        column_panel,
        (((0,), (0,)), ((), ())),
        preferred_element_type=jnp.float32,
    ) * (1.0 / ROWS)
    shard_rows = initial.shape[0]
    col_count = lax.axis_size("col")
    first_feature = (lax.axis_index("row") * col_count + lax.axis_index("col")) * shard_rows
    block_index = (first_feature + jnp.arange(shard_rows, dtype=jnp.int32)) // BLOCK
    selector = (
        block_index[:, None] == jnp.arange(block_mask.shape[0], dtype=jnp.int32)[None, :]
    ).astype(jnp.float32)
    mask_rows = jnp.dot(selector, block_mask.astype(jnp.float32), precision=lax.Precision.HIGHEST)
    mask_full = jnp.repeat(mask_rows, BLOCK, axis=1)
    step_size = ROWS / (D + 2.0 * math.sqrt(D * ROWS) + ROWS)
    current = mask_full * initial
    for iteration in range(ITERS):
        change_now = current - initial
        projected = jnp.dot(
            activations.astype(jnp.float32), change_now, precision=lax.Precision.HIGHEST
        )
        totals = lax.psum(projected, ("row", "col"))
        pulled = lax.dot_general(
            weighted.astype(jnp.float32),
            totals,
            (((0,), (0,)), ((), ())),
            precision=lax.Precision.HIGHEST,
        ) * (1.0 / ROWS)
        current = mask_full * (current - step_size * pulled)
    gram_out = gram_tile.reshape(lax.axis_size("row"), 1, shard_rows, gram_tile.shape[1])
    return (gram_out, current)


def solution(mesh):
    in_specs = (
        P("groups", ("row", "col")),
        P("groups"),
        P(("groups", "row", "col"), None),
        P("groups", None),
    )
    out_specs = (P("groups", "col", None, "row"), P(("groups", "row", "col"), None))
    return jax.shard_map(shards, mesh=mesh, in_specs=in_specs, out_specs=out_specs, check_vma=False)
```

profile of v0, /device:TPU:0, one launch (start us, length us, event | category | flops | bytes accessed | tf_op | source)
XLA Modules:
  0.0 426.7 jit_solution(2539099986985370560)
XLA Ops:
  8.0 0.0 copy-start
  8.0 0.0 copy-start.2
  8.0 0.0 all-reduce.3.cloned.1.call-start
  8.1 1.1 fusion.8
  9.2 0.6 broadcast_in_dim.2
  9.8 4.3 %convolution_bitcast_fusion.1 = f32[1024,256]{0,1:T(8,128)} fusion(bf16[1024,512]{1,0:T(8,128)(2,1)} %param.4, f32[512,256]{1,0:T(8,128)} %param.6, f32[64,8,2,128]{3,2,1,0:T(2,128)S(1)} %bitcast.25), kind=kOutput, calls=%fused_computation.4 | convolution fusion | flops 1610874880 | bytes 3145728 | tf_op jit(solution)/shard_map/dot_general | solution.py:37
  14.1 0.0 all-reduce.3.cloned.1.call-update
  14.1 0.0 all-reduce.5.cloned.1.call-start
  14.1 0.0 copy-done.2
  14.1 0.5 convert_reduce_fusion
  14.7 0.0 copy-done
  14.7 0.3 multiply_convert_fusion
  15.0 0.0 copy-start.1
  15.0 132.6 %all-reduce.3.cloned.1.call-done = f32[1024,256]{0,1:T(8,128)} async-done(((f32[1024,256]{0,1:T(8,128)}), f32[1024,256]{0,1:T(8,128)}) %all-reduce.3.cloned.1.call-update) | async-done | bytes 1048592 | tf_op jit(solution)/shard_map/psum | solution.py:40
  147.6 2.6 fusion.1
  150.3 3.9 convolution_bitcast_fusion
  154.1 0.0 all-reduce.5.cloned.1.call-update
  154.2 0.0 all-gather.5.cloned.1.call-start
  154.2 0.5 all-gather.5.cloned.1.call-update
  154.7 0.0 copy-done.1
  154.7 0.2 all-gather.3.cloned.1.call-start
  155.0 0.4 all-gather.3.cloned.1.call-update
  155.3 234.5 %all-reduce.5.cloned.1.call-done = f32[1024,256]{0,1:T(8,128)} async-done(((f32[1024,256]{0,1:T(8,128)}), f32[1024,256]{0,1:T(8,128)}) %all-reduce.5.cloned.1.call-update) | async-done | bytes 1048592 | tf_op jit(solution)/shard_map/psum | solution.py:40
  389.9 3.6 fusion.3
  393.5 0.0 all-gather.5.cloned.1.call-done
  393.5 0.0 all-gather.3.cloned.1.call-done
  393.5 25.8 %convolution_multiply_fusion = f32[4096,2048]{1,0:T(8,128)} fusion(bf16[1024,4096]{1,0:T(8,128)(2,1)} %all-gather.3.cloned.1.call-done, bf16[1024,2048]{1,0:T(8,128)(2,1)} %all-gather.5.cloned.1.call-done), kind=kOutput, calls=%fused_computation | convolution fusion | flops 17188257792 | bytes 46137344 | tf_op jit(solution)/shard_map/dot_general | solution.py:18
  (2 shorter events, 0.0 us)
Async XLA Ops:
  8.0 6.7 %copy-start = (bf16[1024,512]{1,0:T(8,128)(2,1)S(1)}, bf16[1024,512]{1,0:T(8,128)(2,1)}, u32[]{:S(2)}) copy-start(bf16[1024,512]{1,0:T(8,128)(2,1)} %param.4) | copy-start | bytes 3145732
  8.0 6.1 %copy-start.2 = (s32[1024]{0:T(1024)S(1)}, s32[1024]{0:T(1024)}, u32[]{:S(2)}) copy-start(s32[1024]{0:T(1024)} %param.5) | copy-start | bytes 12292
  8.0 139.6 %all-reduce.3.cloned.1.call-start = ((), (), s32[]{:S(2)}) async-start(), calls=%async_computation.2 | async-start | bytes 2097152 | tf_op jit(solution)/shard_map/psum | solution.py:40
  14.1 375.8 %all-reduce.5.cloned.1.call-start = ((), (), s32[]{:S(2)}) async-start(), calls=%async_computation.3 | async-start | bytes 2097152 | tf_op jit(solution)/shard_map/psum | solution.py:40
  15.0 139.7 %copy-start.1 = (bf16[1024,512]{1,0:T(8,128)(2,1)}, bf16[1024,512]{1,0:T(8,128)(2,1)S(1)}, u32[]{:S(2)}) copy-start(bf16[1024,512]{1,0:T(8,128)(2,1)S(1)} %multiply_convert_fusion) | copy-start | bytes 3145732
  154.2 239.3 %all-gather.5.cloned.1.call-start = ((), (), s32[]{:S(2)}) async-start(), calls=%async_computation.1 | async-start | bytes 5242880 | tf_op jit(solution)/shard_map/all_gather | solution.py:17
  154.7 238.7 %all-gather.3.cloned.1.call-start = ((), (), s32[]{:S(2)}) async-start(), calls=%async_computation | async-start | bytes 9437184 | tf_op jit(solution)/shard_map/all_gather | solution.py:19
Sparse Core Ops, SparseCore 0:
  14.2 133.3 all-reduce.2
  154.3 235.5 all-reduce.4
Sparse Core Ops, SparseCore 1:
  156.2 33.8 all-gather.4
  192.5 125.3 all-gather.2
where the time goes:
time: 427 us
  waiting for transfers between devices  368 us (86%)
  matrix products  41.3 us (10%)
  between operations  15.6 us (4%)
    psum x2, waiting for transfers between devices, shards(): totals = lax.psum(projected, ('row', 'col'))  367 us
    dot_general x1, matrix products, shards(): lax.dot_general(lax.all_gather(weighted, 'row', axis=1, tiled=True), colu...  25.8 us
  transfers between devices with their start and end apart: 4, of which 2 were waited for; matrix products, arithmetic and copies ran while one was open for 1% of the time, Pallas kernels for 0%

commit v1 on v0

--- a/solution.py
+++ b/solution.py
@@ -37,7 +37,7 @@
         projected = jnp.dot(
             activations.astype(jnp.float32), change_now, precision=lax.Precision.HIGHEST
         )
-        totals = lax.psum(projected, ("row", "col"))
+        totals = lax.psum(lax.psum(projected, "row"), axis_name="col")
         pulled = lax.dot_general(
             weighted.astype(jnp.float32),
             totals,

time: 427 us -> 453 us (1.061)
  waiting for transfers between devices: 368 us -> 395 us
    psum x2 -> x4, waiting for transfers between devices: 367 us -> 234 us  [shards(): totals = lax.psum(lax.psum(projected, 'row'), axis_name='col')]
    all_gather x1, waiting for transfers between devices: 0.01 us -> 127 us  [shards(): lax.all_gather(weighted, 'row', axis=1, tiled=True)]
    all_gather x1, waiting for transfers between devices: 0.01 us -> 32.8 us  [shards(): column_panel = lax.all_gather(activations, 'col', axis=1, tiled=True)]
  transfers between devices with their start and end apart: 4 -> 6, of which waited for: 2 -> 6; matrix products, arithmetic and copies ran while one was open for 1% -> 1% of each run, Pallas kernels for 0% -> 0%
where the time goes in v1:
time: 453 us
  waiting for transfers between devices  395 us (87%)
  matrix products  41.2 us (9%)
  between operations  14.2 us (3%)
    psum x4, waiting for transfers between devices, shards(): totals = lax.psum(lax.psum(projected, 'row'), axis_name='col')  234 us
    all_gather x1, waiting for transfers between devices, shards(): lax.all_gather(weighted, 'row', axis=1, tiled=True)  127 us
    all_gather x1, waiting for transfers between devices, shards(): column_panel = lax.all_gather(activations, 'col', axis=1, tiled=True)  32.8 us
    dot_general x1, matrix products, shards(): lax.dot_general(lax.all_gather(weighted, 'row', axis=1, tiled=True), colu...  25.8 us
  transfers between devices with their start and end apart: 6, of which 6 were waited for; matrix products, arithmetic and copies ran while one was open for 1% of the time, Pallas kernels for 0%

profile of v1, /device:TPU:0, one launch (start us, length us, event | category | flops | bytes accessed | tf_op | source)
XLA Modules:
  0.0 452.7 jit_solution(12107221585294015672)
XLA Ops:
  7.2 0.0 copy-start
  7.2 0.0 copy-start.2
  7.2 0.0 all-reduce.5.cloned.1.call-start
  7.3 1.1 fusion.8
  8.3 0.6 broadcast_in_dim.2
  8.9 4.2 convolution_bitcast_fusion.1
  13.2 0.0 all-reduce.5.cloned.1.call-update
  13.2 0.0 all-reduce.7.cloned.1.call-start
  13.2 81.1 %all-reduce.5.cloned.1.call-done = f32[1024,256]{0,1:T(8,128)} async-done(((f32[1024,256]{0,1:T(8,128)}), f32[1024,256]{0,1:T(8,128)}) %all-reduce.5.cloned.1.call-update) | async-done | bytes 1048592 | tf_op jit(solution)/shard_map/psum | solution.py:40
  94.4 0.0 all-reduce.7.cloned.1.call-update
  94.4 0.0 all-reduce.9.cloned.1.call-start
  94.4 0.0 copy-done.2
  94.5 0.5 convert_reduce_fusion
  95.0 0.0 copy-done
  95.0 0.3 multiply_convert_fusion
  95.3 0.0 copy-start.1
  95.3 37.3 %all-reduce.7.cloned.1.call-done = f32[1024,256]{0,1:T(8,128)} async-done(((f32[1024,256]{0,1:T(8,128)}), f32[1024,256]{0,1:T(8,128)}) %all-reduce.7.cloned.1.call-update) | async-done | bytes 1048592 | tf_op jit(solution)/shard_map/psum | solution.py:40
  132.7 2.6 fusion.1
  135.3 3.9 convolution_bitcast_fusion
  139.2 0.0 all-reduce.9.cloned.1.call-update
  139.2 0.0 all-reduce.11.cloned.1.call-start
  139.3 78.9 %all-reduce.9.cloned.1.call-done = f32[1024,256]{0,1:T(8,128)} async-done(((f32[1024,256]{0,1:T(8,128)}), f32[1024,256]{0,1:T(8,128)}) %all-reduce.9.cloned.1.call-update) | async-done | bytes 1048592 | tf_op jit(solution)/shard_map/psum | solution.py:40
  218.1 0.0 all-reduce.11.cloned.1.call-update
  218.2 0.0 copy-done.1
  218.2 0.0 all-gather.5.cloned.1.call-start
  218.2 0.5 all-gather.5.cloned.1.call-update
  218.8 0.2 all-gather.3.cloned.1.call-start
  219.0 0.3 all-gather.3.cloned.1.call-update
  219.3 36.9 %all-reduce.11.cloned.1.call-done = f32[1024,256]{0,1:T(8,128)} async-done(((f32[1024,256]{0,1:T(8,128)}), f32[1024,256]{0,1:T(8,128)}) %all-reduce.11.cloned.1.call-update) | async-done | bytes 1048592 | tf_op jit(solution)/shard_map/psum | solution.py:40
  256.3 3.6 fusion.3
  259.9 32.8 %all-gather.5.cloned.1.call-done = bf16[1024,2048]{1,0:T(8,128)(2,1)} async-done(((bf16[1024,512]{1,0:T(8,128)(2,1)}), bf16[1024,2048]{1,0:T(8,128)(2,1)}) %all-gather.5.cloned.1.call-update) | async-done | bytes 4194320 | tf_op jit(solution)/shard_map/all_gather | solution.py:17
  292.7 127.4 %all-gather.3.cloned.1.call-done = bf16[1024,4096]{1,0:T(8,128)(2,1)} async-done(((bf16[1024,512]{1,0:T(8,128)(2,1)}), bf16[1024,4096]{1,0:T(8,128)(2,1)}) %all-gather.3.cloned.1.call-update) | async-done | bytes 8388624 | tf_op jit(solution)/shard_map/all_gather | solution.py:19
  420.1 25.8 %convolution_multiply_fusion = f32[4096,2048]{1,0:T(8,128)} fusion(bf16[1024,4096]{1,0:T(8,128)(2,1)} %all-gather.3.cloned.1.call-done, bf16[1024,2048]{1,0:T(8,128)(2,1)} %all-gather.5.cloned.1.call-done), kind=kOutput, calls=%fused_computation | convolution fusion | flops 17188257792 | bytes 46137344 | tf_op jit(solution)/shard_map/dot_general | solution.py:18
  (2 shorter events, 0.0 us)
Async XLA Ops:
  7.2 87.8 %copy-start = (bf16[1024,512]{1,0:T(8,128)(2,1)S(1)}, bf16[1024,512]{1,0:T(8,128)(2,1)}, u32[]{:S(2)}) copy-start(bf16[1024,512]{1,0:T(8,128)(2,1)} %param.4) | copy-start | bytes 3145732
  7.2 87.3 %copy-start.2 = (s32[1024]{0:T(1024)S(1)}, s32[1024]{0:T(1024)}, u32[]{:S(2)}) copy-start(s32[1024]{0:T(1024)} %param.5) | copy-start | bytes 12292
  7.2 87.2 %all-reduce.5.cloned.1.call-start = ((), (), s32[]{:S(2)}) async-start(), calls=%async_computation.2 | async-start | bytes 2097152 | tf_op jit(solution)/shard_map/psum | solution.py:40
  13.2 119.5 %all-reduce.7.cloned.1.call-start = ((), (), s32[]{:S(2)}) async-start(), calls=%async_computation.3 | async-start | bytes 2097152 | tf_op jit(solution)/shard_map/psum | solution.py:40
  94.4 123.7 %all-reduce.9.cloned.1.call-start = ((), (), s32[]{:S(2)}) async-start(), calls=%async_computation.4 | async-start | bytes 2097152 | tf_op jit(solution)/shard_map/psum | solution.py:40
  95.3 122.8 %copy-start.1 = (bf16[1024,512]{1,0:T(8,128)(2,1)}, bf16[1024,512]{1,0:T(8,128)(2,1)S(1)}, u32[]{:S(2)}) copy-start(bf16[1024,512]{1,0:T(8,128)(2,1)S(1)} %multiply_convert_fusion) | copy-start | bytes 3145732
  139.2 117.1 %all-reduce.11.cloned.1.call-start = ((), (), s32[]{:S(2)}) async-start(), calls=%async_computation.5 | async-start | bytes 2097152 | tf_op jit(solution)/shard_map/psum | solution.py:40
  218.2 74.5 %all-gather.5.cloned.1.call-start = ((), (), s32[]{:S(2)}) async-start(), calls=%async_computation.1 | async-start | bytes 5242880 | tf_op jit(solution)/shard_map/all_gather | solution.py:17
  218.8 201.3 %all-gather.3.cloned.1.call-start = ((), (), s32[]{:S(2)}) async-start(), calls=%async_computation | async-start | bytes 9437184 | tf_op jit(solution)/shard_map/all_gather | solution.py:19
Sparse Core Ops, SparseCore 0:
  13.3 81.0 all-reduce.4
  96.7 35.8 all-reduce.6
  139.3 78.7 all-reduce.8
  220.4 35.8 all-reduce.10
  257.7 34.9 all-gather.4
  295.1 124.9 all-gather.2
